TPU v7x, 128 devices: a whole 4x4x4 slice. The times are simulated.
128 devices in a mesh: gx: 16 (over z, x), gy: 8 (over y, core).
Axes of the slice: x: 4, y: 4, z: 4, core: 2. Of those that a mesh axis runs over, the one named last changes fastest.
Arguments:
- field: float32 [32, 1024, 1024], P(None, 'gx', 'gy'), may hold values from -6 to 6
- conductivity: float32 [32, 1024, 1024], P(None, 'gx', 'gy'), may hold values from 0.2 to 1
- rate: float32 [32, 1024, 1024], P(None, 'gx', 'gy'), may hold values from 0.05 to 0.5
- patch_cell: int32 [32768], P(('gx', 'gy')), may hold values from 0 to 255
- trainer: int32 [32768, 1], P(('gx', 'gy')), may hold values from 0 to 127; in each aligned block of 256 rows (0 to 255, 256 to 511, ...) at most 4 rows name the same one
- res_slot: int32 [131072], P(('gx', 'gy')), may hold values from 0 to 2047
- reservoir: bfloat16 [262144, 2048], P(('gx', 'gy')), may hold values from -6 to 6
- weights: float32 [2, 1024, 1024], P(None, ('gx', 'gy')), may hold values from -0.1875 to 0.1875
- w_mom: float32 [2, 1024, 1024], P(None, ('gx', 'gy')), may hold values from -0.75 to 0.75
- w_var: float32 [2, 1024, 1024], P(None, ('gx', 'gy')), may hold values from 0.001 to 0.1
- biases: float32 [2, 1024], P(None, ('gx', 'gy')), may hold values from -6 to 6
- b_mom: float32 [2, 1024], P(None, ('gx', 'gy')), may hold values from -0.75 to 0.75
- b_var: float32 [2, 1024], P(None, ('gx', 'gy')), may hold values from 0.001 to 2
Outputs:
- new_field: float32 [32, 1024, 1024], P(None, 'gx', 'gy')
- new_weights: float32 [2, 1024, 1024], P(None, ('gx', 'gy'))
- new_w_mom: float32 [2, 1024, 1024], P(None, ('gx', 'gy'))
- new_w_var: float32 [2, 1024, 1024], P(None, ('gx', 'gy'))
- new_biases: float32 [2, 1024], P(None, ('gx', 'gy'))
- new_b_mom: float32 [2, 1024], P(None, ('gx', 'gy'))
- new_b_var: float32 [2, 1024], P(None, ('gx', 'gy'))
Inputs may be any that keep to these rules, and one draw needn't show every extreme that they name: At most 4 of the patches of one device go to one trainer. `res_slot`: slots of the trainer's own reservoir.
All inputs are finite; a program needn't handle non-finite values.
Results may differ from a plain program's by a relative error of at most 0.0003.
The roundings to bfloat16 on the way count: a program that leaves them out, or rounds other values in their place, can miss the bound.
Values may be sent and summed in bfloat16 or wider, within the bound.
No kernel may reach another device: no remote copies, remote signals or barrier semaphores. Data moves between devices by JAX's collectives and lax.ppermute only.
A program may use at most 128 MiB of HBM per device.

v0:
```python
import jax
import jax.numpy as jnp
from jax import lax
from jax.sharding import PartitionSpec as P

PW = 32
STEPS = 4
time_step = 0.15
learn_rate = 0.001
beta_one = 0.9
beta_two = 0.99
adam_count = 20
tiny_eps = 1e-08


def with_halo(x, sides, width):
    for axis, dim in sides:
        peers, length = (lax.axis_size(axis), x.shape[dim])
        up = [(i, (i + 1) % peers) for i in range(peers - 1)]
        down = [(j, i) for i, j in up]
        last = lax.slice_in_dim(x, length - width, length, axis=dim)
        first = lax.slice_in_dim(x, 0, width, axis=dim)
        before = lax.ppermute(last, axis, up)
        after = lax.ppermute(first, axis, down)
        x = jnp.concatenate([before, x, after], axis=dim)
    return x


def update(padded, kpad, rate_inner):
    inner = slice(1, -1)
    centre = padded[1:-1, 1:-1, 1:-1]
    kcentre = kpad[1:-1, 1:-1, 1:-1]
    sides = [
        (slice(2, None), inner, inner),
        (slice(None, -2), inner, inner),
        (inner, slice(2, None), inner),
        (inner, slice(None, -2), inner),
        (inner, inner, slice(2, None)),
        (inner, inner, slice(None, -2)),
    ]
    flux = jnp.zeros_like(centre)
    for where in sides:
        flux = flux + 0.5 * (kcentre + kpad[where]) * (padded[where] - centre)
    return centre + time_step * (flux - rate_inner * centre)


def zpad(array):
    return jnp.pad(array, ((1, 1), (0, 0), (0, 0)))


def local_grads(rows, live, wbf, bbf):
    width = wbf.shape[1]
    inputs = rows[:, :width]
    target = rows[:, width:].astype(jnp.float32)
    pre = jnp.dot(inputs, wbf[0], preferred_element_type=jnp.float32) + bbf[0].astype(jnp.float32)
    hidden = jnp.tanh(pre)
    hidden_b = hidden.astype(jnp.bfloat16)
    pred = jnp.dot(hidden_b, wbf[1], preferred_element_type=jnp.float32) + bbf[1].astype(
        jnp.float32
    )
    count = jnp.sum(live)
    grad_pred = 2.0 * (pred - target) * live[:, None] / count
    grad_pred_b = grad_pred.astype(jnp.bfloat16)
    grad_w2 = jnp.dot(hidden_b.T, grad_pred_b, preferred_element_type=jnp.float32)
    grad_hid = jnp.dot(grad_pred_b, wbf[1].T, preferred_element_type=jnp.float32)
    grad_pre = grad_hid * (1.0 - hidden * hidden)
    grad_pre_b = grad_pre.astype(jnp.bfloat16)
    grad_w1 = jnp.dot(inputs.T, grad_pre_b, preferred_element_type=jnp.float32)
    return (jnp.stack([grad_w1, grad_w2]), jnp.stack([jnp.sum(grad_pre, 0), jnp.sum(grad_pred, 0)]))


def adam(param, moment, second, grad):
    moment_new = beta_one * moment + (1.0 - beta_one) * grad
    second_new = beta_two * second + (1.0 - beta_two) * grad * grad
    mhat = moment_new / (1.0 - beta_one**adam_count)
    vhat = second_new / (1.0 - beta_two**adam_count)
    return (param - learn_rate * mhat / (jnp.sqrt(vhat) + tiny_eps), moment_new, second_new)


def local(
    field,
    conductivity,
    rate,
    patch_cell,
    trainer,
    res_slot,
    reservoir,
    weights,
    w_mom,
    w_var,
    biases,
    b_mom,
    b_var,
):
    depth, cells_x, cells_y = field.shape
    state = field
    kpad = zpad(with_halo(conductivity, (("gx", 1), ("gy", 2)), 1))
    for step in range(STEPS):
        padded = with_halo(state, (("gx", 1), ("gy", 2)), 1)
        state = update(zpad(padded), kpad, rate)
    devices = lax.axis_size("gx") * lax.axis_size("gy")
    count_dev = patch_cell.shape[0]
    cap = max(2, 2 * count_dev // devices)
    stacked = jnp.stack([field, state]).reshape(2, depth, cells_x * cells_y // PW, PW)
    picked = stacked[:, :, patch_cell, :]
    patches = (
        jnp.transpose(picked, (2, 0, 1, 3)).reshape(count_dev, 2 * depth * PW).astype(jnp.bfloat16)
    )
    target_of = trainer[:, 0]
    onehot = (target_of[:, None] == jnp.arange(devices, dtype=jnp.int32)[None, :]).astype(jnp.int32)
    rank = jnp.sum(jnp.cumsum(onehot, 0) * onehot, 1) - 1
    where_to = target_of * cap + rank
    width2 = patches.shape[1]
    outbox = jnp.zeros((devices * cap, width2), jnp.bfloat16).at[where_to].set(patches)
    flags = (
        jnp.zeros((devices * cap,), jnp.bfloat16)
        .at[where_to]
        .set(jnp.ones((count_dev,), jnp.bfloat16))
    )
    arrived, alive = (
        lax.all_to_all(
            outbox.reshape(devices, cap, width2),
            ("gx", "gy"),
            split_axis=0,
            concat_axis=0,
            tiled=True,
        ),
        lax.all_to_all(
            flags.reshape(devices, cap), ("gx", "gy"), split_axis=0, concat_axis=0, tiled=True
        ),
    )
    arrived = arrived.reshape(devices * cap, width2)
    alive = alive.reshape(devices * cap).astype(jnp.float32)
    wfull, bfull = (
        lax.all_gather(weights.astype(jnp.bfloat16), ("gx", "gy"), axis=1, tiled=True),
        lax.all_gather(biases.astype(jnp.bfloat16), ("gx", "gy"), axis=1, tiled=True),
    )
    rows = jnp.concatenate([reservoir[res_slot], arrived], 0)
    live = jnp.concatenate([jnp.ones((res_slot.shape[0],), jnp.float32), alive])
    grad_w, grad_b = local_grads(rows, live, wfull, bfull)
    share_w, share_b = (
        lax.psum_scatter(grad_w, ("gx", "gy"), scatter_dimension=1, tiled=True),
        lax.psum_scatter(grad_b, ("gx", "gy"), scatter_dimension=1, tiled=True),
    )
    new_w, new_wm, new_wv = adam(weights, w_mom, w_var, share_w)
    new_b, new_bm, new_bv = adam(biases, b_mom, b_var, share_b)
    return (state, new_w, new_wm, new_wv, new_b, new_bm, new_bv)


def solution(mesh):
    return jax.shard_map(
        local,
        mesh=mesh,
        in_specs=(
            P(None, "gx", "gy"),
            P(None, "gx", "gy"),
            P(None, "gx", "gy"),
            P(("gx", "gy")),
            P(("gx", "gy"), None),
            P(("gx", "gy")),
            P(("gx", "gy"), None),
            P(None, ("gx", "gy"), None),
            P(None, ("gx", "gy"), None),
            P(None, ("gx", "gy"), None),
            P(None, ("gx", "gy")),
            P(None, ("gx", "gy")),
            P(None, ("gx", "gy")),
        ),
        out_specs=(
            P(None, "gx", "gy"),
            P(None, ("gx", "gy"), None),
            P(None, ("gx", "gy"), None),
            P(None, ("gx", "gy"), None),
            P(None, ("gx", "gy")),
            P(None, ("gx", "gy")),
            P(None, ("gx", "gy")),
        ),
        check_vma=False,
    )
```

profile of v0, /device:TPU:0, one launch (start us, length us, event | category | flops | bytes accessed | tf_op | source)
XLA Modules:
  0.0 1021.7 jit_solution(17814061396416684958)
XLA Ops:
  14.0 4.5 collective-permute-start.4
  34.5 5.4 collective-permute-start.6
  56.2 5.1 fusion.73
  62.7 5.2 collective-permute-start.8
  91.3 5.1 fusion.55
  102.2 4.3 collective-permute-done.13
  124.9 22.5 %all-to-all-start.1 = ((bf16[128,1,4]{2,1,0:T(2,128)(2,1)}), bf16[128,1,4]{2,1,0:T(2,128)(2,1)}, u32[]{:S(2)}, u32[]{:S(2)}) async-start(bf16[128,1,4]{2,1,0:T(2,128)(2,1)} %all_to_all.12), calls=%async_computation.1 | async-start | bytes 131072 | tf_op jit(solution)/shard_map/all_to_all | solution.py:128
  155.5 5.1 fusion.37
  178.0 12.3 %collective-permute-start.19 = (f32[32,66,1]{1,0,2:T(8,128)}, f32[32,66,1]{1,0,2:T(8,128)}, u32[]{:S(2)}, u32[]{:S(2)}) collective-permute-start(f32[32,66,1]{1,0,2:T(8,128)} %copy.255), channel_id=1, source_target_pairs={{1,0},{2,1},{3,2},{4,3},{5,4},{6,5},{7,6},{9,8},{10,9},{11,10},{12... | collective-permute-start | bytes 25352 | tf_op jit(solution)/shard_map/ppermute | solution.py:24
  195.3 4.3 copy.264
  207.7 5.8 fusion.19
  220.7 5.4 gather_fusion.1
  226.2 4.9 copy.266
  236.9 14.4 %all-to-all-start = ((bf16[128,4,2048]{2,1,0:T(4,128)(2,1)}), bf16[128,4,2048]{2,1,0:T(4,128)(2,1)S(1)}, u32[]{:S(2)}, u32[]{:S(2)}) async-start(bf16[128,4,2048]{2,1,0:T(4,128)(2,1)} %reshape.62), calls=%async_computation | async-start | bytes 4194304 | tf_op jit(solution)/shard_map/all_to_all | solution.py:121
  251.4 49.2 %all-gather = bf16[128,8,2]{1,2,0:T(2,128)(2,1)S(1)} all-gather(bf16[1,8,2]{1,2,0:T(2,128)(2,1)S(1)} %convert_bitcast_fusion), channel_id=1, replica_groups=mesh['gx'=16,'gy'=8] {'gx','gy'}, dimensions={0}, use_global_device_ids=true | all-gather | bytes 4128 | tf_op jit(solution)/shard_map/all_gather | solution.py:136
  300.8 13.5 %gather_fusion = bf16[1024,2048]{1,0:T(8,128)(2,1)} fusion(bf16[2048,2048]{1,0:T(8,128)(2,1)} %param.19, s32[1024]{0:T(1024)S(1)} %copy-done.58), kind=kCustom, calls=%fused_computation | custom fusion | bytes 8392704 | tf_op jit(solution)/shard_map/gather | solution.py:138
  314.3 4.8 constant_dynamic-update-slice_fusion.1
  326.1 6.2 fusion.4
  332.3 4.8 fusion.121
  340.7 6.2 fusion.122
  346.8 5.5 fusion.7
  352.4 4.2 pad_maximum_fusion.1
  356.6 64.3 %all-reduce.6 = f32[2,1024]{1,0:T(2,128)S(1)} all-reduce(f32[2,1024]{1,0:T(2,128)S(1)} %pad_maximum_fusion.47), channel_id=3, replica_groups=mesh['gx'=16,'gy'=8] {'gx','gy'}, use_global_device_ids=true, to_apply=%region_9.10.clone | all-reduce | flops 2048 | bytes 16384
  421.6 591.2 %reduce-scatter.3.cloned.1.call-done = f32[2,8,1024]{2,1,0:T(8,128)} async-done(((f32[2,1024,1024]{2,1,0:T(8,128)}), f32[2,8,1024]{2,1,0:T(8,128)}) %reduce-scatter.3.cloned.1.call-update) | async-done | bytes 65552 | tf_op jit(solution)/shard_map/reduce_scatter | solution.py:142
  (252 shorter events, 151.9 us)
Async XLA Ops:
  7.2 318.9 %all-gather.3.cloned.1.call-start = ((), (), s32[]{:S(2)}) async-start(), calls=%async_computation.3 | async-start | bytes 4227072 | tf_op jit(solution)/shard_map/all_gather | solution.py:135
  8.2 14.2 %collective-permute-start = (f32[32,1,128]{2,0,1:T(8,128)S(1)}, f32[32,1,128]{2,0,1:T(8,128)S(1)}, u32[]{:S(2)}, u32[]{:S(2)}) collective-permute-start(f32[32,1,128]{2,0,1:T(8,128)S(1)} %bitcast.121), channel_id=1, source_target_pairs={{0,8},{8,16},{16,24},{24,32},{32,40},{40,48},{48,56},{56,64},{64,7... | collective-permute-start | bytes 49160 | tf_op jit(solution)/shard_map/ppermute | solution.py:23
  11.7 10.7 %collective-permute-start.1 = (f32[32,1,128]{2,0,1:T(8,128)S(1)}, f32[32,1,128]{2,0,1:T(8,128)S(1)}, u32[]{:S(2)}, u32[]{:S(2)}) collective-permute-start(f32[32,1,128]{2,0,1:T(8,128)S(1)} %bitcast.120), channel_id=1, source_target_pairs={{8,0},{16,8},{24,16},{32,24},{40,32},{48,40},{56,48},{64,56},{72,6... | collective-permute-start | bytes 49160 | tf_op jit(solution)/shard_map/ppermute | solution.py:24
  14.0 16.5 %collective-permute-start.4 = (f32[32,1,128]{2,0,1:T(8,128)S(1)}, f32[32,1,128]{2,0,1:T(8,128)S(1)}, u32[]{:S(2)}, u32[]{:S(2)}) collective-permute-start(f32[32,1,128]{2,0,1:T(8,128)S(1)} %bitcast.119), channel_id=1, source_target_pairs={{0,8},{8,16},{16,24},{24,32},{32,40},{40,48},{48,56},{56,64},{64,7... | collective-permute-start | bytes 49160 | tf_op jit(solution)/shard_map/ppermute | solution.py:23
  18.6 12.0 %collective-permute-start.5 = (f32[32,1,128]{2,0,1:T(8,128)S(1)}, f32[32,1,128]{2,0,1:T(8,128)S(1)}, u32[]{:S(2)}, u32[]{:S(2)}) collective-permute-start(f32[32,1,128]{2,0,1:T(8,128)S(1)} %bitcast.118), channel_id=1, source_target_pairs={{8,0},{16,8},{24,16},{32,24},{40,32},{48,40},{56,48},{64,56},{72,6... | collective-permute-start | bytes 49160 | tf_op jit(solution)/shard_map/ppermute | solution.py:24
  27.5 14.8 %collective-permute-start.2 = (f32[32,66,1]{1,0,2:T(8,128)S(1)}, f32[32,66,1]{1,0,2:T(8,128)S(1)}, u32[]{:S(2)}, u32[]{:S(2)}) collective-permute-start(f32[32,66,1]{1,0,2:T(8,128)S(1)} %copy.206), channel_id=1, source_target_pairs={{0,1},{1,2},{2,3},{3,4},{4,5},{5,6},{6,7},{8,9},{9,10},{10,11},{11... | collective-permute-start | bytes 25352 | tf_op jit(solution)/shard_map/ppermute | solution.py:23
  29.2 14.6 %collective-permute-start.3 = (f32[32,66,1]{1,0,2:T(8,128)S(1)}, f32[32,66,1]{1,0,2:T(8,128)S(1)}, u32[]{:S(2)}, u32[]{:S(2)}) collective-permute-start(f32[32,66,1]{1,0,2:T(8,128)S(1)} %copy.207), channel_id=1, source_target_pairs={{1,0},{2,1},{3,2},{4,3},{5,4},{6,5},{7,6},{9,8},{10,9},{11,10},{12... | collective-permute-start | bytes 25352 | tf_op jit(solution)/shard_map/ppermute | solution.py:24
  34.5 13.6 %collective-permute-start.6 = (f32[32,66,1]{1,0,2:T(8,128)}, f32[32,66,1]{1,0,2:T(8,128)}, u32[]{:S(2)}, u32[]{:S(2)}) collective-permute-start(f32[32,66,1]{1,0,2:T(8,128)} %copy.214), channel_id=1, source_target_pairs={{0,1},{1,2},{2,3},{3,4},{4,5},{5,6},{6,7},{8,9},{9,10},{10,11},{11... | collective-permute-start | bytes 25352 | tf_op jit(solution)/shard_map/ppermute | solution.py:23
  41.0 9.4 collective-permute-start.7
  61.4 7.2 collective-permute-start.9
  62.7 6.6 collective-permute-start.8
  74.1 9.0 collective-permute-start.10
  79.9 5.4 collective-permute-start.11
  96.4 5.8 collective-permute-start.12
  100.3 6.2 collective-permute-start.13
  111.3 36.0 %collective-permute-start.14 = (f32[32,66,1]{1,0,2:T(8,128)}, f32[32,66,1]{1,0,2:T(8,128)}, u32[]{:S(2)}, u32[]{:S(2)}) collective-permute-start(f32[32,66,1]{1,0,2:T(8,128)} %copy.242), channel_id=1, source_target_pairs={{0,1},{1,2},{2,3},{3,4},{4,5},{5,6},{6,7},{8,9},{9,10},{10,11},{11... | collective-permute-start | bytes 25352 | tf_op jit(solution)/shard_map/ppermute | solution.py:23
  117.5 32.1 %collective-permute-start.15 = (f32[32,66,1]{1,0,2:T(8,128)}, f32[32,66,1]{1,0,2:T(8,128)}, u32[]{:S(2)}, u32[]{:S(2)}) collective-permute-start(f32[32,66,1]{1,0,2:T(8,128)} %copy.243), channel_id=1, source_target_pairs={{1,0},{2,1},{3,2},{4,3},{5,4},{6,5},{7,6},{9,8},{10,9},{11,10},{12... | collective-permute-start | bytes 25352 | tf_op jit(solution)/shard_map/ppermute | solution.py:24
  124.9 112.1 %all-to-all-start.1 = ((bf16[128,1,4]{2,1,0:T(2,128)(2,1)}), bf16[128,1,4]{2,1,0:T(2,128)(2,1)}, u32[]{:S(2)}, u32[]{:S(2)}) async-start(bf16[128,1,4]{2,1,0:T(2,128)(2,1)} %all_to_all.12), calls=%async_computation.1 | async-start | bytes 131072 | tf_op jit(solution)/shard_map/all_to_all | solution.py:128
  160.6 4.7 collective-permute-start.16
  163.4 5.6 collective-permute-start.17
  173.8 25.7 %collective-permute-start.18 = (f32[32,66,1]{1,0,2:T(8,128)}, f32[32,66,1]{1,0,2:T(8,128)}, u32[]{:S(2)}, u32[]{:S(2)}) collective-permute-start(f32[32,66,1]{1,0,2:T(8,128)} %copy.254), channel_id=1, source_target_pairs={{0,1},{1,2},{2,3},{3,4},{4,5},{5,6},{6,7},{8,9},{9,10},{10,11},{11... | collective-permute-start | bytes 25352 | tf_op jit(solution)/shard_map/ppermute | solution.py:23
  178.0 23.8 %collective-permute-start.19 = (f32[32,66,1]{1,0,2:T(8,128)}, f32[32,66,1]{1,0,2:T(8,128)}, u32[]{:S(2)}, u32[]{:S(2)}) collective-permute-start(f32[32,66,1]{1,0,2:T(8,128)} %copy.255), channel_id=1, source_target_pairs={{1,0},{2,1},{3,2},{4,3},{5,4},{6,5},{7,6},{9,8},{10,9},{11,10},{12... | collective-permute-start | bytes 25352 | tf_op jit(solution)/shard_map/ppermute | solution.py:24
  236.9 83.9 %all-to-all-start = ((bf16[128,4,2048]{2,1,0:T(4,128)(2,1)}), bf16[128,4,2048]{2,1,0:T(4,128)(2,1)S(1)}, u32[]{:S(2)}, u32[]{:S(2)}) async-start(bf16[128,4,2048]{2,1,0:T(4,128)(2,1)} %reshape.62), calls=%async_computation | async-start | bytes 4194304 | tf_op jit(solution)/shard_map/all_to_all | solution.py:121
  251.4 761.5 %reduce-scatter.3.cloned.1.call-start = ((), (), s32[]{:S(2)}) async-start(), calls=%async_computation.4 | async-start | bytes 8454144 | tf_op jit(solution)/shard_map/reduce_scatter | solution.py:142
  (67 other events, 2431.5 us)
Sparse Core Ops, SparseCore 0:
  21.5 72.0 all-gather.2
  356.7 656.1 reduce-scatter.2
where the time goes:
time: 1030 us; the launch traced here: 1020 us
  waiting for transfers between devices  600 us (58%)
  blocking collectives  114 us (11%)
  local copies, waits for them, and re-layouts  113 us (11%)
  starting transfers between devices  96.9 us (9%)
  other arithmetic  56.5 us (5%)
  matrix products  26.3 us (3%)
  between operations  15.5 us (2%)
    reduce_scatter x1, waiting for transfers between devices, local(): lax.psum_scatter(grad_w, ('gx', 'gy'), scatter_dimension=1, tiled=True)  591 us
    unnamed x1, blocking collectives  64.3 us
    all_gather x1, blocking collectives, local(): lax.all_gather(biases.astype(jnp.bfloat16), ('gx', 'gy'), axis=1, tiled=T...  49.2 us
    ppermute x10, starting transfers between devices, with_halo(): before = lax.ppermute(last, axis, up)  35.8 us
    ppermute x10, starting transfers between devices, with_halo(): after = lax.ppermute(first, axis, down)  24.1 us
    all_to_all x1, starting transfers between devices, local(): lax.all_to_all(flags.reshape(devices, cap), ('gx', 'gy'), split_axis=0, c...  22.5 us
    add x4, other arithmetic, update(): return centre + time_step * (flux - rate_inner * centre)  21 us
  transfers between devices with their start and end apart: 24, of which 4 were waited for; matrix products, arithmetic and copies ran while one was open for 15% of the time, Pallas kernels for 0%

commit v1 on v0

--- a/solution.py
+++ b/solution.py
@@ -11,6 +11,11 @@
 beta_two = 0.99
 adam_count = 20
 tiny_eps = 1e-08
+
+
+def exchange_gather(x, mesh_axis, dim):
+    sent = jnp.stack([x] * lax.axis_size(mesh_axis))
+    return jnp.concatenate(lax.all_to_all(sent, mesh_axis, 0, 0), axis=dim)
 
 
 def with_halo(x, sides, width):
@@ -133,7 +138,7 @@
     alive = alive.reshape(devices * cap).astype(jnp.float32)
     wfull, bfull = (
         lax.all_gather(weights.astype(jnp.bfloat16), ("gx", "gy"), axis=1, tiled=True),
-        lax.all_gather(biases.astype(jnp.bfloat16), ("gx", "gy"), axis=1, tiled=True),
+        exchange_gather(biases.astype(jnp.bfloat16), ("gx", "gy"), 1),
     )
     rows = jnp.concatenate([reservoir[res_slot], arrived], 0)
     live = jnp.concatenate([jnp.ones((res_slot.shape[0],), jnp.float32), alive])

time: 1030 us -> 984 us (0.955)
  blocking collectives: 114 us -> 63.2 us
    all_gather x1 -> x0, blocking collectives: 49.2 us -> none  [local(): lax.all_gather(biases.astype(jnp.bfloat16), ('gx', 'gy'), axis=1, tiled=T...]
    all_to_all x0 -> x1, starting transfers between devices: none -> 14.4 us  [exchange_gather(): return jnp.concatenate(lax.all_to_all(sent, mesh_axis, 0, 0), axis=dim)]
    ppermute x10, starting transfers between devices: 24.1 us -> 13.5 us  [with_halo(): after = lax.ppermute(first, axis, down)]
  transfers between devices with their start and end apart: 24 -> 25, of which waited for: 4 -> 5; matrix products, arithmetic and copies ran while one was open for 15% -> 16% of each run, Pallas kernels for 0% -> 0%
where the time goes in v1:
time: 984 us; the launch traced here: 975 us
  waiting for transfers between devices  607 us (62%)
  local copies, waits for them, and re-layouts  110 us (11%)
  starting transfers between devices  96.2 us (10%)
  blocking collectives  63.2 us (6%)
  other arithmetic  59.6 us (6%)
  matrix products  23.1 us (2%)
  between operations  15.3 us (2%)
    reduce_scatter x1, waiting for transfers between devices, local(): lax.psum_scatter(grad_w, ('gx', 'gy'), scatter_dimension=1, tiled=True)  589 us
    unnamed x1, blocking collectives  63.2 us
    ppermute x10, starting transfers between devices, with_halo(): before = lax.ppermute(last, axis, up)  36 us
    all_to_all x1, starting transfers between devices, local(): lax.all_to_all(flags.reshape(devices, cap), ('gx', 'gy'), split_axis=0, c...  22.3 us
    add x4, other arithmetic, update(): return centre + time_step * (flux - rate_inner * centre)  21.1 us
  transfers between devices with their start and end apart: 25, of which 5 were waited for; matrix products, arithmetic and copies ran while one was open for 16% of the time, Pallas kernels for 0%

profile of v1, /device:TPU:0, one launch (start us, length us, event | category | flops | bytes accessed | tf_op | source)
XLA Modules:
  0.0 974.8 jit_solution(16518857602788616627)
XLA Ops:
  14.0 4.5 collective-permute-start.4
  30.6 5.4 collective-permute-start.6
  52.4 5.1 fusion.73
  58.8 5.2 collective-permute-start.8
  86.7 5.1 fusion.55
  98.0 4.3 collective-permute-done.13
  120.6 22.3 %all-to-all-start.2 = ((bf16[128,1,4]{2,1,0:T(2,128)(2,1)}), bf16[128,1,4]{2,1,0:T(2,128)(2,1)}, u32[]{:S(2)}, u32[]{:S(2)}) async-start(bf16[128,1,4]{2,1,0:T(2,128)(2,1)} %all_to_all.16), calls=%async_computation.2 | async-start | bytes 131072 | tf_op jit(solution)/shard_map/all_to_all | solution.py:133
  151.1 5.1 fusion.37
  179.8 4.3 copy.259
  192.8 5.8 fusion.19
  204.8 14.4 %all-to-all-start.1 = ((bf16[128,2,8]{2,1,0:T(2,128)(2,1)}), bf16[128,2,8]{2,1,0:T(2,128)(2,1)S(1)}, u32[]{:S(2)}, u32[]{:S(2)}) async-start(bf16[128,2,8]{2,1,0:T(2,128)(2,1)} %stack.23), calls=%async_computation.1 | async-start | bytes 131072 | tf_op jit(solution)/shard_map/all_to_all | solution.py:18
  219.2 5.2 pad_maximum_fusion
  224.4 5.5 gather_fusion.1
  229.9 4.9 copy.261
  240.6 9.8 %all-to-all-start = ((bf16[128,4,2048]{2,1,0:T(4,128)(2,1)}), bf16[128,4,2048]{2,1,0:T(4,128)(2,1)S(1)}, u32[]{:S(2)}, u32[]{:S(2)}) async-start(bf16[128,4,2048]{2,1,0:T(4,128)(2,1)} %reshape.86), calls=%async_computation | async-start | bytes 4194304 | tf_op jit(solution)/shard_map/all_to_all | solution.py:126
  250.6 13.3 %gather_fusion = bf16[1024,2048]{1,0:T(8,128)(2,1)} fusion(bf16[2048,2048]{1,0:T(8,128)(2,1)} %param.19, s32[1024]{0:T(1024)S(1)} %copy-done.57), kind=kCustom, calls=%fused_computation | custom fusion | bytes 8392704 | tf_op jit(solution)/shard_map/gather | solution.py:143
  263.9 4.8 constant_dynamic-update-slice_fusion.1
  271.0 9.7 all-to-all-done
  286.0 6.2 fusion.4
  292.2 4.8 fusion.123
  300.6 5.0 fusion.124
  309.2 4.2 pad_maximum_fusion.1
  313.4 63.2 %all-reduce.6 = f32[2,1024]{1,0:T(2,128)S(1)} all-reduce(f32[2,1024]{1,0:T(2,128)S(1)} %pad_maximum_fusion.47), channel_id=3, replica_groups=mesh['gx'=16,'gy'=8] {'gx','gy'}, use_global_device_ids=true, to_apply=%region_9.10.clone | all-reduce | flops 2048 | bytes 16384
  377.4 588.9 %reduce-scatter.3.cloned.1.call-done = f32[2,8,1024]{2,1,0:T(8,128)} async-done(((f32[2,1024,1024]{2,1,0:T(8,128)}), f32[2,8,1024]{2,1,0:T(8,128)}) %reduce-scatter.3.cloned.1.call-update) | async-done | bytes 65552 | tf_op jit(solution)/shard_map/reduce_scatter | solution.py:147
  (256 shorter events, 152.6 us)
Async XLA Ops:
  7.2 278.9 %all-gather.2.cloned.1.call-start = ((), (), s32[]{:S(2)}) async-start(), calls=%async_computation.4 | async-start | bytes 4227072 | tf_op jit(solution)/shard_map/all_gather | solution.py:140
  8.2 14.9 %collective-permute-start = (f32[32,1,128]{2,0,1:T(8,128)S(1)}, f32[32,1,128]{2,0,1:T(8,128)S(1)}, u32[]{:S(2)}, u32[]{:S(2)}) collective-permute-start(f32[32,1,128]{2,0,1:T(8,128)S(1)} %bitcast.113), channel_id=1, source_target_pairs={{0,8},{8,16},{16,24},{24,32},{32,40},{40,48},{48,56},{56,64},{64,7... | collective-permute-start | bytes 49160 | tf_op jit(solution)/shard_map/ppermute | solution.py:28
  11.7 11.3 %collective-permute-start.1 = (f32[32,1,128]{2,0,1:T(8,128)S(1)}, f32[32,1,128]{2,0,1:T(8,128)S(1)}, u32[]{:S(2)}, u32[]{:S(2)}) collective-permute-start(f32[32,1,128]{2,0,1:T(8,128)S(1)} %bitcast.112), channel_id=1, source_target_pairs={{8,0},{16,8},{24,16},{32,24},{40,32},{48,40},{56,48},{64,56},{72,6... | collective-permute-start | bytes 49160 | tf_op jit(solution)/shard_map/ppermute | solution.py:29
  14.0 14.9 %collective-permute-start.4 = (f32[32,1,128]{2,0,1:T(8,128)S(1)}, f32[32,1,128]{2,0,1:T(8,128)S(1)}, u32[]{:S(2)}, u32[]{:S(2)}) collective-permute-start(f32[32,1,128]{2,0,1:T(8,128)S(1)} %bitcast.111), channel_id=1, source_target_pairs={{0,8},{8,16},{16,24},{24,32},{32,40},{40,48},{48,56},{56,64},{64,7... | collective-permute-start | bytes 49160 | tf_op jit(solution)/shard_map/ppermute | solution.py:28
  18.6 10.3 %collective-permute-start.5 = (f32[32,1,128]{2,0,1:T(8,128)S(1)}, f32[32,1,128]{2,0,1:T(8,128)S(1)}, u32[]{:S(2)}, u32[]{:S(2)}) collective-permute-start(f32[32,1,128]{2,0,1:T(8,128)S(1)} %bitcast.110), channel_id=1, source_target_pairs={{8,0},{16,8},{24,16},{32,24},{40,32},{48,40},{56,48},{64,56},{72,6... | collective-permute-start | bytes 49160 | tf_op jit(solution)/shard_map/ppermute | solution.py:29
  25.9 12.5 %collective-permute-start.2 = (f32[32,66,1]{1,0,2:T(8,128)S(1)}, f32[32,66,1]{1,0,2:T(8,128)S(1)}, u32[]{:S(2)}, u32[]{:S(2)}) collective-permute-start(f32[32,66,1]{1,0,2:T(8,128)S(1)} %copy.201), channel_id=1, source_target_pairs={{0,1},{1,2},{2,3},{3,4},{4,5},{5,6},{6,7},{8,9},{9,10},{10,11},{11... | collective-permute-start | bytes 25352 | tf_op jit(solution)/shard_map/ppermute | solution.py:28
  27.6 12.3 %collective-permute-start.3 = (f32[32,66,1]{1,0,2:T(8,128)S(1)}, f32[32,66,1]{1,0,2:T(8,128)S(1)}, u32[]{:S(2)}, u32[]{:S(2)}) collective-permute-start(f32[32,66,1]{1,0,2:T(8,128)S(1)} %copy.202), channel_id=1, source_target_pairs={{1,0},{2,1},{3,2},{4,3},{5,4},{6,5},{7,6},{9,8},{10,9},{11,10},{12... | collective-permute-start | bytes 25352 | tf_op jit(solution)/shard_map/ppermute | solution.py:29
  30.6 13.6 %collective-permute-start.6 = (f32[32,66,1]{1,0,2:T(8,128)}, f32[32,66,1]{1,0,2:T(8,128)}, u32[]{:S(2)}, u32[]{:S(2)}) collective-permute-start(f32[32,66,1]{1,0,2:T(8,128)} %copy.209), channel_id=1, source_target_pairs={{0,1},{1,2},{2,3},{3,4},{4,5},{5,6},{6,7},{8,9},{9,10},{10,11},{11... | collective-permute-start | bytes 25352 | tf_op jit(solution)/shard_map/ppermute | solution.py:28
  37.1 9.4 collective-permute-start.7
  57.5 7.2 collective-permute-start.9
  58.8 6.6 collective-permute-start.8
  69.7 8.8 collective-permute-start.10
  75.4 5.4 collective-permute-start.11
  91.9 6.0 collective-permute-start.12
  96.1 6.2 collective-permute-start.13
  107.1 35.8 %collective-permute-start.14 = (f32[32,66,1]{1,0,2:T(8,128)}, f32[32,66,1]{1,0,2:T(8,128)}, u32[]{:S(2)}, u32[]{:S(2)}) collective-permute-start(f32[32,66,1]{1,0,2:T(8,128)} %copy.237), channel_id=1, source_target_pairs={{0,1},{1,2},{2,3},{3,4},{4,5},{5,6},{6,7},{8,9},{9,10},{10,11},{11... | collective-permute-start | bytes 25352 | tf_op jit(solution)/shard_map/ppermute | solution.py:28
  113.3 31.9 %collective-permute-start.15 = (f32[32,66,1]{1,0,2:T(8,128)}, f32[32,66,1]{1,0,2:T(8,128)}, u32[]{:S(2)}, u32[]{:S(2)}) collective-permute-start(f32[32,66,1]{1,0,2:T(8,128)} %copy.238), channel_id=1, source_target_pairs={{1,0},{2,1},{3,2},{4,3},{5,4},{6,5},{7,6},{9,8},{10,9},{11,10},{12... | collective-permute-start | bytes 25352 | tf_op jit(solution)/shard_map/ppermute | solution.py:29
  120.6 83.5 %all-to-all-start.2 = ((bf16[128,1,4]{2,1,0:T(2,128)(2,1)}), bf16[128,1,4]{2,1,0:T(2,128)(2,1)}, u32[]{:S(2)}, u32[]{:S(2)}) async-start(bf16[128,1,4]{2,1,0:T(2,128)(2,1)} %all_to_all.16), calls=%async_computation.2 | async-start | bytes 131072 | tf_op jit(solution)/shard_map/all_to_all | solution.py:133
  159.0 5.6 collective-permute-start.17
  168.9 15.7 %collective-permute-start.18 = (f32[32,66,1]{1,0,2:T(8,128)}, f32[32,66,1]{1,0,2:T(8,128)}, u32[]{:S(2)}, u32[]{:S(2)}) collective-permute-start(f32[32,66,1]{1,0,2:T(8,128)} %copy.249), channel_id=1, source_target_pairs={{0,1},{1,2},{2,3},{3,4},{4,5},{5,6},{6,7},{8,9},{9,10},{10,11},{11... | collective-permute-start | bytes 25352 | tf_op jit(solution)/shard_map/ppermute | solution.py:28
  173.1 13.8 %collective-permute-start.19 = (f32[32,66,1]{1,0,2:T(8,128)}, f32[32,66,1]{1,0,2:T(8,128)}, u32[]{:S(2)}, u32[]{:S(2)}) collective-permute-start(f32[32,66,1]{1,0,2:T(8,128)} %copy.250), channel_id=1, source_target_pairs={{1,0},{2,1},{3,2},{4,3},{5,4},{6,5},{7,6},{9,8},{10,9},{11,10},{12... | collective-permute-start | bytes 25352 | tf_op jit(solution)/shard_map/ppermute | solution.py:29
  204.8 35.8 %all-to-all-start.1 = ((bf16[128,2,8]{2,1,0:T(2,128)(2,1)}), bf16[128,2,8]{2,1,0:T(2,128)(2,1)S(1)}, u32[]{:S(2)}, u32[]{:S(2)}) async-start(bf16[128,2,8]{2,1,0:T(2,128)(2,1)} %stack.23), calls=%async_computation.1 | async-start | bytes 131072 | tf_op jit(solution)/shard_map/all_to_all | solution.py:18
  240.6 40.1 %all-to-all-start = ((bf16[128,4,2048]{2,1,0:T(4,128)(2,1)}), bf16[128,4,2048]{2,1,0:T(4,128)(2,1)S(1)}, u32[]{:S(2)}, u32[]{:S(2)}) async-start(bf16[128,4,2048]{2,1,0:T(4,128)(2,1)} %reshape.86), calls=%async_computation | async-start | bytes 4194304 | tf_op jit(solution)/shard_map/all_to_all | solution.py:126
  250.4 715.8 %reduce-scatter.3.cloned.1.call-start = ((), (), s32[]{:S(2)}) async-start(), calls=%async_computation.5 | async-start | bytes 8454144 | tf_op jit(solution)/shard_map/reduce_scatter | solution.py:147
  (69 other events, 2423.0 us)
Sparse Core Ops, SparseCore 0:
  21.5 72.0 all-gather.1
  313.5 652.6 reduce-scatter.2
